TPU v7x, 256 devices: a whole 4x4x8 slice. The times are simulated.
256 devices in a mesh: rep: 8 (over x, z_hi), seq: 4 (over y), tp: 8 (over z_lo, core).
Axes of the slice: x: 4, y: 4, z: 8 (z_hi: 2, z_lo: 4; z = z_hi * 4 + z_lo), core: 2. Of those that a mesh axis runs over, the one named last changes fastest.
Arguments:
- hidden_in: bfloat16 [32768, 1536], P(('rep', 'seq', 'tp')), may hold values from -3 to 3
- routes: int32 [32768, 4], P(('rep', 'seq', 'tp')), may hold values from 0 to 31, all different within a row; in each aligned block of 128 rows (0 to 127, 128 to 255, ...) at most 24 rows name the same one
- prefix_len: int32 [8], replicated, may hold values from 256 to 2048, as said below
- cache: bfloat16 [8, 2, 2048, 256], P(None, None, ('rep', 'seq')), may hold values from -400 to 400, as said below
- attn_gain: float32 [1536], replicated, may hold values from 0.1 to 1.9
- w_query: bfloat16 [1536, 1024], P(None, 'tp'), may hold values from -0.375 to 0.375
- w_keyval: bfloat16 [2, 1536, 256], replicated, may hold values from -0.15625 to 0.15625
- w_out: bfloat16 [1024, 1536], P('tp'), may hold values from -0.375 to 0.375
- moe_gain: float32 [1536], replicated, may hold values from 0.1 to 1.9
- w_router: bfloat16 [1536, 32], replicated, may hold values from -0.15625 to 0.15625
- expert_in: bfloat16 [32, 1536, 1536], P(('seq', 'tp')), may hold values from -0.15625 to 0.15625
- expert_out: bfloat16 [32, 768, 1536], P(('seq', 'tp')), may hold values from -0.875 to 0.875
Outputs:
- hidden_out: bfloat16 [32768, 1536], P(('rep', 'seq', 'tp'))
- new_cache: bfloat16 [32768, 512], P(('rep', 'seq'), 'tp')
Inputs may be any that keep to these rules, and one draw needn't show every extreme that they name: `routes`: each row names 4 different experts; within the rows of one device (aligned blocks of 128 rows) no expert is named by more than 24 rows. prefix_len[r] cached positions (0 to prefix_len[r] - 1) of request r are valid; some request has 2048. cache[r, g, p, 0:128] is a key, cache[r, g, p, 128:] a value.
All inputs are finite; a program needn't handle non-finite values.
Results may differ from a plain program's by a relative error of at most 0.029.
The roundings to bfloat16 on the way count: a program that leaves them out, or rounds other values in their place, can miss the bound.
Values may be sent and summed in bfloat16 or wider, within the bound.
No kernel may reach another device: no remote copies, remote signals or barrier semaphores. Data moves between devices by JAX's collectives and lax.ppermute only.
A program may use at most 64 MiB of HBM per device.

v0:
```python
import jax
import jax.numpy as jnp
from jax import lax
from jax.sharding import PartitionSpec as P

CAP = 24


epsilon = 1e-06
masked_score = -1e30


def rms_scale(rows, gain):
    values = rows.astype(jnp.float32)
    inverse = lax.rsqrt(jnp.mean(values * values, axis=-1, keepdims=True) + epsilon)
    return (values * inverse * gain).astype(jnp.bfloat16)


def attend(state, query_rows, block, visible, scale):
    best, total, summed = state
    head_dim = block.shape[1] // 2
    scores = (
        lax.dot_general(
            query_rows,
            block[:, :head_dim],
            (((1,), (1,)), ((), ())),
            preferred_element_type=jnp.float32,
        )
        * scale
    )
    scores = jnp.where(visible, scores, masked_score)
    new_best = jnp.maximum(best, jnp.max(scores, axis=1))
    weights = jnp.where(visible, jnp.exp(scores - new_best[:, None]), 0.0)
    factor = jnp.exp(best - new_best)
    total = total * factor + jnp.sum(weights, axis=1)
    summed = summed * factor[:, None] + jnp.dot(
        weights.astype(jnp.bfloat16), block[:, head_dim:], preferred_element_type=jnp.float32
    )
    return (new_best, total, summed)


def body(
    hidden_in,
    routes,
    prefix_len,
    cache,
    attn_gain,
    w_query,
    w_keyval,
    w_out,
    moe_gain,
    w_router,
    expert_in,
    expert_out,
):
    tp_count = lax.axis_size("tp")
    seq_count = lax.axis_size("seq")
    rep_count = lax.axis_size("rep")
    tp_index = lax.axis_index("tp")
    seq_index = lax.axis_index("seq")
    rep_index = lax.axis_index("rep")
    rows_dev, width = hidden_in.shape
    kv_heads = w_keyval.shape[0]
    pair_cols = w_keyval.shape[2]
    head_dim = pair_cols // 2
    query_cols = w_query.shape[1]
    heads_dev = query_cols // head_dim
    piece_len = rows_dev * tp_count
    scale = 1.0 / float(head_dim) ** 0.5
    kv_index = tp_index // (tp_count // kv_heads)
    normed = rms_scale(hidden_in, attn_gain)
    head_weight = lax.dynamic_index_in_dim(w_keyval, kv_index, 0, keepdims=False)
    joined = jnp.concatenate([w_query, head_weight], axis=1)
    projected = jnp.dot(
        lax.all_gather(normed, "tp", axis=0, tiled=True), joined, preferred_element_type=jnp.float32
    ).astype(jnp.bfloat16)
    count_rows = piece_len * heads_dev
    query_rows = projected[:, :query_cols]
    fresh = projected[:, query_cols:]
    col_width = kv_heads * pair_cols // tp_count
    new_cache = lax.dynamic_slice_in_dim(fresh, tp_index * col_width % pair_cols, col_width, 1)
    own_pages = lax.dynamic_index_in_dim(cache, kv_index, 1, keepdims=True)
    fetched = lax.all_to_all(own_pages, "rep", split_axis=0, concat_axis=2, tiled=True)
    page_rows = fetched.shape[2]
    pages = fetched.reshape(page_rows, pair_cols)
    page_len = page_rows // rep_count
    length = lax.dynamic_index_in_dim(prefix_len, rep_index, 0, keepdims=False)
    row_ids = jnp.arange(page_rows, dtype=jnp.int32)

    def page_visible(source):
        position = (row_ids // page_len * seq_count + source) * page_len + row_ids % page_len
        return (position < length)[None, :]

    def fresh_visible(source, query_piece):
        token = jnp.arange(count_rows, dtype=jnp.int32) // heads_dev + query_piece * piece_len
        key_pos = source * piece_len + jnp.arange(piece_len, dtype=jnp.int32)
        return key_pos[None, :] <= token[:, None]

    start_state = (
        jnp.full((count_rows,), masked_score, jnp.float32),
        jnp.zeros((count_rows,), jnp.float32),
        jnp.zeros((count_rows, head_dim), jnp.float32),
    )
    shard_rows = page_rows + piece_len
    local_keys = jnp.concatenate([pages, fresh], axis=0)

    def fold_shard(state, shard, source):
        state = attend(state, query_rows, shard[:page_rows], page_visible(source), scale)

        def with_fresh(inner):
            return attend(
                inner, query_rows, shard[page_rows:], fresh_visible(source, seq_index), scale
            )

        return lax.cond(source <= seq_index, with_fresh, lambda inner: inner, state)

    state = start_state
    gathered = lax.all_gather(local_keys, "seq", axis=0, tiled=True)
    count = gathered.shape[0] // shard_rows
    shards = gathered.reshape(count, shard_rows, pair_cols)

    def advance(inner, item):
        offset, shard = item
        return (fold_shard(inner, shard, offset), None)

    state, _ = lax.scan(advance, state, (jnp.arange(count, dtype=jnp.int32), shards))
    best, total, summed = state
    attended = (summed / total[:, None]).astype(jnp.bfloat16)
    rows = attended
    head_total = lax.psum_scatter(
        jnp.dot(rows, w_out, preferred_element_type=jnp.float32),
        "tp",
        scatter_dimension=0,
        tiled=True,
    )
    mid = (hidden_in.astype(jnp.float32) + head_total).astype(jnp.bfloat16)
    normed_moe = rms_scale(mid, moe_gain)
    experts_all = w_router.shape[1]
    top = routes.shape[1]
    expert_ids = jnp.arange(experts_all, dtype=jnp.int32)
    logits = jnp.dot(normed_moe, w_router, preferred_element_type=jnp.float32)
    matches = routes[:, :, None] == expert_ids[None, None, :]
    chosen = jnp.sum(jnp.where(matches, logits[:, None, :], 0.0), axis=2)
    raised = jnp.exp(chosen)
    gates = raised / jnp.sum(raised, axis=1, keepdims=True)
    flat_routes = routes.reshape(rows_dev * top)
    onehot = (flat_routes[:, None] == expert_ids[None, :]).astype(jnp.int32)
    before = jnp.cumsum(onehot, axis=0) - onehot
    slot = jnp.sum(before * onehot, axis=1)
    target = flat_routes * CAP + slot
    outgoing = (
        jnp.zeros((experts_all * CAP, width), jnp.bfloat16)
        .at[target]
        .set(jnp.repeat(normed_moe, top, axis=0))
    )
    group_count = seq_count * tp_count
    local_experts = expert_in.shape[0]
    inner_dim = expert_out.shape[1]
    arrived = lax.all_to_all(
        outgoing.reshape(group_count, local_experts, CAP, width),
        ("seq", "tp"),
        split_axis=0,
        concat_axis=0,
        tiled=True,
    )
    rows = arrived[:, 0].reshape(-1, width)
    inner = jnp.dot(rows, expert_in[0], preferred_element_type=jnp.float32)
    active = (jnp.maximum(inner[:, :inner_dim], 0.0) * inner[:, inner_dim:]).astype(jnp.bfloat16)
    output = jnp.dot(active, expert_out[0], preferred_element_type=jnp.float32).astype(jnp.bfloat16)
    results = [output.reshape(arrived.shape[0], arrived.shape[2], width)]
    returned = lax.all_to_all(
        jnp.stack(results, axis=1), ("seq", "tp"), split_axis=0, concat_axis=0, tiled=True
    )
    picked = returned.reshape(experts_all * CAP, width)[target].reshape(rows_dev, top, width)
    mixed = jnp.sum(gates[:, :, None] * picked.astype(jnp.float32), axis=1)
    hidden_out = (mid.astype(jnp.float32) + mixed).astype(jnp.bfloat16)
    return (hidden_out, new_cache)


def solution(mesh):
    placed = (
        P(("rep", "seq", "tp"), None),
        P(("rep", "seq", "tp"), None),
        P(),
        P(None, None, ("rep", "seq"), None),
        P(),
        P(None, "tp"),
        P(),
        P("tp", None),
        P(),
        P(),
        P(("seq", "tp"), None, None),
        P(("seq", "tp"), None, None),
    )
    return jax.shard_map(
        body,
        mesh=mesh,
        in_specs=placed,
        out_specs=(P(("rep", "seq", "tp"), None), P(("rep", "seq"), "tp")),
        check_vma=False,
    )
```

profile of v0, /device:TPU:1, one launch (start us, length us, event | category | flops | bytes accessed | tf_op | source)
XLA Modules:
  0.0 418.8 jit_solution(9488731846069213498)
XLA Ops:
  7.2 1.3 fusion.57
  8.6 1.9 fusion.59
  10.5 1.7 constant_dynamic-slice_fusion.2
  12.2 11.5 %all-to-all-start = ((bf16[8,1,64,256]{3,2,1,0:T(8,128)(2,1)}), bf16[8,1,64,256]{3,2,1,0:T(8,128)(2,1)S(1)}, u32[]{:S(2)}, u32[]{:S(2)}) async-start(bf16[8,1,64,256]{3,2,1,0:T(8,128)(2,1)} %constant_dynamic-slice_fusion.2), calls=%async_computation | async-start | bytes 524288 | tf_op jit(solution)/shard_map/all_to_all | solution.py:83
  23.7 2.1 dynamic-slice_bitcast_fusion.1
  25.8 8.2 %all-to-all-done = bf16[8,1,64,256]{3,2,1,0:T(8,128)(2,1)S(1)} async-done(((bf16[8,1,64,256]{3,2,1,0:T(8,128)(2,1)}), bf16[8,1,64,256]{3,2,1,0:T(8,128)(2,1)S(1)}, u32[]{:S(2)}, u32[]{:S(2)}) %all-to-all-start) | async-done | bytes 262176 | tf_op jit(solution)/shard_map/all_to_all | solution.py:83
  34.2 26.8 %all-gather.3.cloned.1.call-done = bf16[1024,1536]{1,0:T(8,128)(2,1)} async-done(((bf16[128,1536]{1,0:T(8,128)(2,1)}), bf16[1024,1536]{1,0:T(8,128)(2,1)}) %all-gather.3.cloned.1.call-update) | async-done | bytes 3145744 | tf_op jit(solution)/shard_map/all_gather | solution.py:75
  61.0 3.5 convolution_convert_fusion.1
  64.5 0.9 copy-done.3
  65.4 0.8 copy-done.2
  66.2 1.0 pad_maximum_fusion
  67.4 0.7 dynamic_slice.33
  68.1 1.0 slice.75
  69.2 41.3 %all-gather.5.cloned.1.call-done = bf16[6144,256]{0,1:T(8,128)(2,1)} async-done(((bf16[1536,256]{0,1:T(8,128)(2,1)}), bf16[6144,256]{0,1:T(8,128)(2,1)}) %all-gather.5.cloned.1.call-update) | async-done | bytes 3145744 | tf_op jit(solution)/shard_map/all_gather | solution.py:118
  110.6 4.6 %copy.48 = bf16[6144,256]{1,0:T(8,128)(2,1)} copy(bf16[6144,256]{0,1:T(8,128)(2,1)} %all-gather.5.cloned.1.call-done) | data formatting | bytes 6291456
  115.2 0.8 broadcast_in_dim.92
  116.0 39.8 %while.20 = (s32[]{:T(128)}, f32[1024]{0:T(1024)S(1)}, f32[1024]{0:T(1024)S(1)}, f32[1024,128]{1,0:T(8,128)}, s32[4]{0:T(128)S(1)}, /*index=5*/s32[]{:T(128)}, s...) while((s32[]{:T(128)}, f32[1024]{0:T(1024)S(1)}, ...), condition=%wide.region_8.9_spmd.clone.clone, body=%wide.region_1.8_spmd.clone.clone.sunk | while | flops 829438464 | bytes 24546600 | solution.py:126
  116.0 0.6 dynamic_slice.48
  117.2 1.3 fusion.91
  118.5 1.0 dynamic-slice_bitcast_fusion.3
  119.5 1.2 constant_dynamic-slice_fusion.4
  121.1 0.6 fusion.93
  121.7 2.7 convolution_add_fusion.2
  124.4 6.2 %conditional.4 = ((f32[1024]{0:T(1024)S(1)}, f32[1024]{0:T(1024)S(1)}, f32[1024,128]{1,0:T(8,128)})) conditional(s32[]{:T(128)} %convert_element_type.129, (f32[1024]{0:T(1024)S(1)}, f32[1024]{0:T(1024)S(1)}, f32[1024,128]{1,0:T(8,128)}) %tuple.70, (s32[]{:T(128)}, s32[]{:T(128)}, bf16[1,1536,256]{2,1,0:T(8,128)(2,1)S(1)}, ...), branch_computations={%region_4.4_spmd, %region_5.7_spmd} | conditional | flops 553914368 | bytes 14516288 | solution.py:115
  125.0 0.8 fusion.8
  125.8 1.5 fusion.10
  127.4 3.3 fusion.13
  130.6 0.6 dynamic_slice.48
  131.8 1.3 fusion.91
  133.1 1.0 dynamic-slice_bitcast_fusion.3
  134.1 1.2 constant_dynamic-slice_fusion.4
  135.7 0.6 fusion.93
  136.3 2.7 convolution_add_fusion.2
  139.0 0.6 dynamic_slice.48
  140.2 1.3 fusion.91
  141.5 1.0 dynamic-slice_bitcast_fusion.3
  142.5 1.2 constant_dynamic-slice_fusion.4
  144.1 0.6 fusion.93
  144.7 2.7 convolution_add_fusion.2
  147.4 0.6 dynamic_slice.48
  148.6 1.3 fusion.91
  149.9 1.0 dynamic-slice_bitcast_fusion.3
  150.9 1.2 constant_dynamic-slice_fusion.4
  152.1 0.5 fusion.92
  152.5 0.6 fusion.93
  153.1 2.7 convolution_add_fusion.2
  155.8 4.8 %fusion.65 = f32[1024,1536]{1,0:T(8,128)} fusion(bf16[128,1536]{1,0:T(8,128)(2,1)} %param.23, f32[1024,128]{1,0:T(8,128)} %get-tuple-element.277, f32[1024]{0:T(1024)S(1)} %get-tuple-element.278), kind=kOutput, calls=%fused_computation.89 | convolution fusion | flops 402915328 | bytes 7213056 | tf_op jit(solution)/shard_map/dot_general | solution.py:131
  160.7 0.7 copy-done.5
  162.0 1.2 reduce-window.6
  163.5 87.9 %reduce-scatter.2.cloned.1.call-done = f32[128,1536]{1,0:T(8,128)} async-done(((f32[1024,1536]{1,0:T(8,128)}), f32[128,1536]{1,0:T(8,128)}) %reduce-scatter.2.cloned.1.call-update) | async-done | bytes 786448 | tf_op jit(solution)/shard_map/reduce_scatter | solution.py:130
  251.5 1.3 fusion.61
  253.0 1.6 broadcast_in_dim.96
  254.5 3.7 reshape.208
  258.2 5.5 %scatter_custom_fusion = bf16[768,1536]{1,0:T(8,128)(2,1)} fusion(s32[512]{0:T(512)S(1)} %bitcast.64, bf16[512,1536]{1,0:T(8,128)(2,1)} %reshape.208, bf16[]{:T(256)} %constant.204.clone.1), kind=kCustom, calls=%fused_computation.76 | custom fusion | bytes 2359808 | tf_op jit(solution)/shard_map/scatter | solution.py:154
  263.8 63.9 %all_to_all.19 = bf16[32,1,24,1536]{3,2,1,0:T(8,128)(2,1)S(1)} all-to-all(bf16[32,1,24,1536]{3,2,1,0:T(8,128)(2,1)} %bitcast.60), channel_id=1, replica_groups=mesh['rep'=8,'seq'=4,'tp'=8] {'seq','tp'}, dimensions={0} | all-to-all | bytes 4718592 | tf_op jit(solution)/shard_map/all_to_all | solution.py:159
  327.7 5.7 %fusion.46 = f32[768,1536]{1,0:T(8,128)S(1)} fusion(bf16[768,1536]{1,0:T(8,128)(2,1)S(1)} %bitcast.62, bf16[1,1536,1536]{2,1,0:T(8,128)(2,1)} %param.26), kind=kOutput, calls=%fused_computation.57 | convolution fusion | flops 3623878656 | bytes 11796480 | tf_op jit(solution)/shard_map/dot_general | solution.py:167
  333.4 3.4 convolution_convert_fusion
  336.7 4.7 %all-to-all-start.2 = ((bf16[32,1,24,1536]{3,2,1,0:T(8,128)(2,1)}), bf16[32,1,24,1536]{3,2,1,0:T(8,128)(2,1)}, u32[]{:S(2)}, u32[]{:S(2)}) async-start(bf16[32,1,24,1536]{3,2,1,0:T(8,128)(2,1)} %bitcast.61), calls=%async_computation.3 | async-start | bytes 4718592 | tf_op jit(solution)/shard_map/all_to_all | solution.py:171
  341.5 1.6 constant_dynamic-slice_fusion.1
  343.5 53.2 %all-to-all-done.2 = bf16[32,1,24,1536]{3,2,1,0:T(8,128)(2,1)} async-done(((bf16[32,1,24,1536]{3,2,1,0:T(8,128)(2,1)}), bf16[32,1,24,1536]{3,2,1,0:T(8,128)(2,1)}, u32[]{:S(2)}, u32[]{:S(2)}) %all-to-all-start.2) | async-done | bytes 2359328 | tf_op jit(solution)/shard_map/all_to_all | solution.py:171
  396.7 6.4 %gather_fusion = bf16[512,1536]{1,0:T(8,128)(2,1)} fusion(bf16[768,1536]{1,0:T(8,128)(2,1)} %bitcast.14, s32[1024]{0:T(1024)S(1)} %pad_clamp_fusion), kind=kCustom, calls=%fused_computation | custom fusion | bytes 3147776 | tf_op jit(solution)/shard_map/gather | solution.py:174
  403.1 4.2 %reshape.195 = f32[128,4,1536]{2,1,0:T(4,128)} reshape(bf16[512,1536]{1,0:T(8,128)(2,1)} %gather_fusion) | data formatting | bytes 4718592 | tf_op jit(solution)/shard_map/convert_element_type | solution.py:175
  407.3 4.2 multiply_reduce_fusion
  411.5 0.8 fusion.64
  (74 shorter events, 3.8 us)
Async XLA Ops:
  7.2 326.2 %copy-start = (bf16[1,768,1536]{2,1,0:T(8,128)(2,1)S(1)}, bf16[1,768,1536]{2,1,0:T(8,128)(2,1)}, u32[]{:S(2)}) copy-start(bf16[1,768,1536]{2,1,0:T(8,128)(2,1)} %param.27) | copy-start | bytes 7077892
  7.2 53.8 %copy-start.7 = (bf16[1536,128]{1,0:T(8,128)(2,1)S(1)}, bf16[1536,128]{1,0:T(8,128)(2,1)}, u32[]{:S(2)}) copy-start(bf16[1536,128]{1,0:T(8,128)(2,1)} %param.21) | copy-start | bytes 1179652
  7.2 53.8 %all-gather.3.cloned.1.call-start = ((), (), s32[]{:S(2)}) async-start(), calls=%async_computation.4 | async-start | bytes 3538944 | tf_op jit(solution)/shard_map/all_gather | solution.py:75
  12.2 21.8 %all-to-all-start = ((bf16[8,1,64,256]{3,2,1,0:T(8,128)(2,1)}), bf16[8,1,64,256]{3,2,1,0:T(8,128)(2,1)S(1)}, u32[]{:S(2)}, u32[]{:S(2)}) async-start(bf16[8,1,64,256]{3,2,1,0:T(8,128)(2,1)} %constant_dynamic-slice_fusion.2), calls=%async_computation | async-start | bytes 524288 | tf_op jit(solution)/shard_map/all_to_all | solution.py:83
  23.7 86.9 %all-gather.5.cloned.1.call-start = ((), (), s32[]{:S(2)}) async-start(), calls=%async_computation.5 | async-start | bytes 3932160 | tf_op jit(solution)/shard_map/all_gather | solution.py:118
  64.5 0.9 copy-start.3
  65.4 2.1 copy-start.8
  65.4 0.8 copy-start.2
  67.2 184.3 %reduce-scatter.2.cloned.1.call-start = ((), (), s32[]{:S(2)}) async-start(), calls=%async_computation.6 | async-start | bytes 7077888 | tf_op jit(solution)/shard_map/reduce_scatter | solution.py:130
  160.7 0.7 copy-start.5
  160.7 90.8 %copy-start.1 = (bf16[128,1536]{1,0:T(8,128)(2,1)S(1)}, bf16[128,1536]{1,0:T(8,128)(2,1)}, u32[]{:S(2)}) copy-start(bf16[128,1536]{1,0:T(8,128)(2,1)} %param.16) | copy-start | bytes 1179652
  160.7 92.1 %copy-start.6 = (f32[1536]{0:T(1024)S(1)}, f32[1536]{0:T(1024)}, u32[]{:S(2)}) copy-start(f32[1536]{0:T(1024)} %param.24) | copy-start | bytes 18436
  336.7 6.3 %copy-start.4 = (bf16[1536,32]{0,1:T(8,128)(2,1)S(1)}, bf16[1536,32]{0,1:T(8,128)(2,1)}, u32[]{:S(2)}) copy-start(bf16[1536,32]{0,1:T(8,128)(2,1)} %param.25) | copy-start | bytes 294916
  336.7 60.0 %all-to-all-start.2 = ((bf16[32,1,24,1536]{3,2,1,0:T(8,128)(2,1)}), bf16[32,1,24,1536]{3,2,1,0:T(8,128)(2,1)}, u32[]{:S(2)}, u32[]{:S(2)}) async-start(bf16[32,1,24,1536]{3,2,1,0:T(8,128)(2,1)} %bitcast.61), calls=%async_computation.3 | async-start | bytes 4718592 | tf_op jit(solution)/shard_map/all_to_all | solution.py:171
Sparse Core Ops, SparseCore 0:
  10.6 50.3 all-gather.2
  67.3 43.2 all-gather.4
  160.8 90.5 reduce-scatter.1
where the time goes:
time: 421 us; the launch traced here: 419 us
  waiting for transfers between devices  218 us (52%)
  blocking collectives  63.9 us (15%)
  local copies, waits for them, and re-layouts  48.4 us (11%)
  matrix products  34.3 us (8%)
  other arithmetic  21.2 us (5%)
  starting transfers between devices  16.5 us (4%)
  between operations  14 us (3%)
    reduce_scatter x1, waiting for transfers between devices, body(): lax.psum_scatter(jnp.dot(rows, w_out, preferred_element_type=jnp.float32)...  87.9 us
    all_to_all x1, blocking collectives, body(): lax.all_to_all(outgoing.reshape(group_count, local_experts, CAP, width),...  63.9 us
    all_to_all x1, waiting for transfers between devices, body(): lax.all_to_all(jnp.stack(results, axis=1), ('seq', 'tp'), split_axis=0, c...  53.2 us
    all_gather x1, waiting for transfers between devices, body(): gathered = lax.all_gather(local_keys, 'seq', axis=0, tiled=True)  41.3 us
    all_gather x1, waiting for transfers between devices, body(): lax.all_gather(normed, 'tp', axis=0, tiled=True)  26.8 us
    dot_general x5, matrix products, attend(): jnp.dot(weights.astype(jnp.bfloat16), block[:, head_dim:], preferred_elem...  14.1 us
    all_to_all x1, starting transfers between devices, body(): lax.all_to_all(own_pages, 'rep', split_axis=0, concat_axis=2, tiled=True)  11.5 us
  transfers between devices with their start and end apart: 5, of which 5 were waited for; matrix products, arithmetic and copies ran while one was open for 2% of the time, Pallas kernels for 0%

commit v1 on v0

v1 whole, which is shorter than its diff:
```python
import jax
import jax.numpy as jnp
from jax import lax
from jax.experimental import pallas as pl
from jax.experimental.pallas import tpu as pltpu
from jax.sharding import Mesh
from jax.sharding import PartitionSpec as P

CAP = 24
epsilon = 1e-06
masked_score = -1e30
log2e = 1.4426950408889634

X, ZH, Y, ZL, C = 4, 2, 4, 4, 2


def rms_scale(rows, gain):
    values = rows.astype(jnp.float32)
    inverse = lax.rsqrt(jnp.mean(values * values, axis=-1, keepdims=True) + epsilon)
    return (values * inverse * gain).astype(jnp.bfloat16)


def swap_core(a):
    return lax.ppermute(a, "c", [(0, 1), (1, 0)])


def shift_line(a, s):
    return lax.ppermute(a, "zl", [(i, (i + s) % ZL) for i in range(ZL)])


def shift_y(a, s):
    pairs = []
    for y in range(Y):
        for c in range(C):
            t = (y + (s if c == 0 else -s)) % Y
            pairs.append((y * C + c, t * C + c))
    return lax.ppermute(a, ("y", "c"), pairs)


def attention_kernel(
    meta, q_ref, own_ref, a_ref, b_ref, f_ref, o_ref, qs, m_ref, l_ref, acc_ref, *, pages, fresh
):
    rows = qs.shape[0]
    heads = rows // 256
    scale = log2e / float(128) ** 0.5
    y, zl, c, length = meta[0], meta[1], meta[2], meta[3]
    for s in range(heads):
        h = lax.rem(zl - s + 4, 4)
        qs[s * 256 : (s + 1) * 256, :] = q_ref[:, pl.ds(pl.multiple_of(h * 128, 128), 128)]

    def scores_of(keys):
        return (
            lax.dot_general(
                qs[...], keys, (((1,), (1,)), ((), ())), preferred_element_type=jnp.float32
            )
            * scale
        )

    def fold(scores, values):
        old = m_ref[...]
        new = jnp.maximum(old, jnp.max(scores, axis=1, keepdims=True))
        m_ref[...] = new
        weights = jnp.exp2(scores - new[:, :1])
        factor = jnp.exp2(old - new)
        l_ref[...] = l_ref[...] * factor + jnp.sum(weights, axis=1, keepdims=True)
        acc_ref[...] = acc_ref[...] * factor + jnp.dot(
            weights.astype(jnp.bfloat16), values, preferred_element_type=jnp.float32
        )

    m_ref[...] = jnp.full(m_ref.shape, masked_score, jnp.float32)
    l_ref[...] = jnp.zeros(l_ref.shape, jnp.float32)
    acc_ref[...] = jnp.zeros(acc_ref.shape, jnp.float32)

    def half_of(index):
        return ((index % 256) // 128) * (1 - 2 * c) + c

    key = lax.broadcasted_iota(jnp.int32, (1, fresh), 1)
    key_chip = (zl - key // 256 + 4) % 4
    key_pos = key_chip * 256 + half_of(key) * 128 + key % 128
    row = lax.broadcasted_iota(jnp.int32, (rows, 1), 0)
    row_pos = zl * 256 + half_of(row) * 128 + row % 128
    scores = scores_of(own_ref[pages:, :128])
    scores = jnp.where(key_pos <= row_pos, scores, masked_score)
    fold(scores, own_ref[pages:, 128:])

    step = 1 - 2 * c
    shards = ((own_ref, y), (a_ref, y - step), (b_ref, y + step), (f_ref, y + 2))
    page = lax.broadcasted_iota(jnp.int32, (1, pages), 1)
    for ref, source in shards:
        source = lax.rem(source + 4, 4)
        position = (page // 64 * 4 + source) * 64 + page % 64
        scores = scores_of(ref[:pages, :128])
        scores = jnp.where(position < length, scores, masked_score)
        fold(scores, ref[:pages, 128:])
        if ref is not own_ref:

            @pl.when(source < y)
            def _(ref=ref):
                fold(scores_of(ref[pages:, :128]), ref[pages:, 128:])

    done = (acc_ref[...] / l_ref[...]).astype(o_ref.dtype)
    for s in range(heads):
        o_ref[:, s * 128 : (s + 1) * 128] = done[s * 256 : (s + 1) * 256, :]


def order_kernel(meta, x_ref, o_ref):
    zl, c = meta[1], meta[2]
    col = pl.multiple_of(lax.rem(zl, 2) * 128, 128)
    for z in range(ZL):
        slot = lax.rem(zl - z + 4, 4)
        for half in range(2):
            inner = half * (1 - 2 * c) + c
            start = pl.multiple_of(slot * 256 + inner * 128, 128)
            o_ref[z * 256 + half * 128 : z * 256 + half * 128 + 128, :] = x_ref[
                pl.ds(start, 128), pl.ds(col, 128)
            ]


def body(
    hidden_in,
    routes,
    prefix_len,
    cache,
    attn_gain,
    w_query,
    w_keyval,
    w_out,
    moe_gain,
    w_router,
    expert_in,
    expert_out,
):
    y, zl, c = lax.axis_index("y"), lax.axis_index("zl"), lax.axis_index("c")
    rep = lax.axis_index(("x", "zh"))
    rows_dev, width = hidden_in.shape
    length = lax.dynamic_index_in_dim(prefix_len, rep, 0, keepdims=False)
    meta = jnp.stack([y, zl, c, length]).astype(jnp.int32)
    smem = pl.BlockSpec(memory_space=pltpu.SMEM)
    vmem = pl.BlockSpec(memory_space=pltpu.VMEM)

    group_size = 4
    with jax.named_scope("weights"):
        wq_all = lax.all_gather(w_query, ("zl", "c"), axis=0, tiled=False)
        to_group = []
        for z in range(ZL):
            for k in range(C):
                to_group.append((z * C + k, (2 * (z % 2) + k) * C + z // 2))
        wo_here = lax.ppermute(w_out, ("zl", "c"), to_group)
        wo = jnp.concatenate([wo_here] + [shift_line(wo_here, s) for s in (1, 2, 3)], axis=0)

    with jax.named_scope("pages"):
        own_pages = lax.dynamic_index_in_dim(cache, c, 1, keepdims=True)
        fetched = lax.all_to_all(own_pages, ("x", "zh"), split_axis=0, concat_axis=2, tiled=True)
        pages = fetched.reshape(-1, 256)

    with jax.named_scope("keys"):
        normed = rms_scale(hidden_in, attn_gain)
        both = jnp.concatenate([normed, swap_core(normed)], axis=0)
        w_kv = lax.dynamic_index_in_dim(w_keyval, c, 0, keepdims=False)
        kv = jnp.dot(both, w_kv, preferred_element_type=jnp.float32).astype(jnp.bfloat16)
        line = [kv] + [shift_line(kv, s) for s in (1, 2, 3)]
        shard = jnp.concatenate([pages] + line, axis=0)
        up = shift_y(shard, 1)
        down = shift_y(shard, -1)
        far = shift_y(up, 1)

    with jax.named_scope("new_cache"):
        ordered = pl.pallas_call(
            order_kernel,
            out_shape=jax.ShapeDtypeStruct((1024, 128), jnp.bfloat16),
            in_specs=[smem, vmem],
            out_specs=vmem,
        )(meta, jnp.concatenate(line, axis=0))
        other = swap_core(ordered)
        held = jnp.where(c == zl // 2, ordered, other)
        new_cache = jnp.where(c == 0, held[:, :64], held[:, 64:])

    with jax.named_scope("queries"):
        wq = lax.dynamic_slice_in_dim(wq_all, c * group_size, group_size, 0)
        queries = jnp.concatenate(
            [jnp.dot(both, wq[h], preferred_element_type=jnp.float32) for h in range(group_size)],
            axis=1,
        ).astype(jnp.bfloat16)

    with jax.named_scope("attention"):
        n_pages = pages.shape[0]
        n_rows = 2 * rows_dev * group_size
        attended = pl.pallas_call(
            lambda *refs: attention_kernel(*refs, pages=n_pages, fresh=1024),
            out_shape=jax.ShapeDtypeStruct((2 * rows_dev, group_size * 128), jnp.bfloat16),
            in_specs=[smem] + [vmem] * 5,
            out_specs=vmem,
            scratch_shapes=[
                pltpu.VMEM((n_rows, 128), jnp.bfloat16),
                pltpu.VMEM((n_rows, 128), jnp.float32),
                pltpu.VMEM((n_rows, 128), jnp.float32),
                pltpu.VMEM((n_rows, 128), jnp.float32),
            ],
            compiler_params=pltpu.CompilerParams(vmem_limit_bytes=48 * 2**20),
            cost_estimate=pl.CostEstimate(
                flops=4 * n_rows * 6144 * 128,
                bytes_accessed=4 * 2**20,
                transcendentals=n_rows * 6144,
            ),
            name="attention",
        )(meta, queries, shard, up, down, far)

    with jax.named_scope("out_projection"):
        partial = jnp.dot(attended, wo, preferred_element_type=jnp.float32)
        received = swap_core(partial[rows_dev:])
        mid = (hidden_in.astype(jnp.float32) + (partial[:rows_dev] + received)).astype(jnp.bfloat16)
        normed_moe = rms_scale(mid, moe_gain)

    with jax.named_scope("routing"):
        experts_all = w_router.shape[1]
        top = routes.shape[1]
        slots = experts_all * CAP
        expert_ids = jnp.arange(experts_all, dtype=jnp.int32)
        matches = routes[:, :, None] == expert_ids[None, None, :]
        named = jnp.sum(matches.astype(jnp.float32), axis=1)
        lower = (
            jnp.arange(rows_dev)[:, None] > jnp.arange(rows_dev)[None, :]
        ).astype(jnp.float32)
        before = jnp.dot(lower, named, preferred_element_type=jnp.float32)
        slot = jnp.sum(jnp.where(matches, before[:, None, :], 0.0), axis=2).astype(jnp.int32)
        target = routes * CAP + slot
        slot_ids = jnp.arange(slots, dtype=jnp.int32)
        placed = sum((target[:, k : k + 1] == slot_ids[None, :]) for k in range(top)).astype(
            jnp.bfloat16
        )

    with jax.named_scope("dispatch"):
        outgoing = lax.dot_general(
            placed, normed_moe, (((0,), (0,)), ((), ())), preferred_element_type=jnp.float32
        ).astype(jnp.bfloat16)
        arrived = lax.all_to_all(
            outgoing.reshape(experts_all, CAP, width),
            ("y", "zl", "c"),
            split_axis=0,
            concat_axis=0,
            tiled=True,
        )

    with jax.named_scope("gates"):
        logits = jnp.dot(normed_moe, w_router, preferred_element_type=jnp.float32)
        chosen = jnp.sum(jnp.where(matches, logits[:, None, :], 0.0), axis=2)
        raised = jnp.exp(chosen)
        gates = raised / jnp.sum(raised, axis=1, keepdims=True)
        mix = sum(
            jnp.where(target[:, k : k + 1] == slot_ids[None, :], gates[:, k : k + 1], 0.0)
            for k in range(top)
        )
        mix_high = mix.astype(jnp.bfloat16)
        mix_low = (mix - mix_high.astype(jnp.float32)).astype(jnp.bfloat16)
        mix_both = jnp.concatenate([mix_high, mix_low], axis=0)

    with jax.named_scope("experts"):
        inner_dim = expert_out.shape[1]
        inner = jnp.dot(
            arrived.reshape(slots, width), expert_in[0], preferred_element_type=jnp.float32
        )
        active = (jnp.maximum(inner[:, :inner_dim], 0.0) * inner[:, inner_dim:]).astype(
            jnp.bfloat16
        )
        output = jnp.dot(active, expert_out[0], preferred_element_type=jnp.float32).astype(
            jnp.bfloat16
        )

    with jax.named_scope("combine"):
        returned = lax.all_to_all(
            output.reshape(experts_all, CAP, width),
            ("y", "zl", "c"),
            split_axis=0,
            concat_axis=0,
            tiled=True,
        ).reshape(slots, width)
        mixed = jnp.dot(mix_both, returned, preferred_element_type=jnp.float32)
        hidden_out = (mid.astype(jnp.float32) + (mixed[:rows_dev] + mixed[rows_dev:])).astype(
            jnp.bfloat16
        )
    return (hidden_out, new_cache)


def solution(mesh):
    axes = ("x", "zh", "y", "zl", "c")
    split = Mesh(mesh.devices.reshape(X, ZH, Y, ZL, C), axes)
    placed = (
        P(axes, None),
        P(axes, None),
        P(),
        P(None, None, ("x", "zh", "y"), None),
        P(),
        P(None, ("zl", "c")),
        P(),
        P(("zl", "c"), None),
        P(),
        P(),
        P(("y", "zl", "c"), None, None),
        P(("y", "zl", "c"), None, None),
    )
    return jax.shard_map(
        body,
        mesh=split,
        in_specs=placed,
        out_specs=(P(axes, None), P(("x", "zh", "y"), ("zl", "c"))),
        check_vma=False,
    )
```

time: 421 us -> 263 us (0.62)
  waiting for transfers between devices: 218 us -> 101 us
  local copies, waits for them, and re-layouts: 48.4 us -> 3.19 us
  starting transfers between devices: 16.5 us -> 42.5 us
  other arithmetic: 21.2 us -> 6.2 us
  matrix products: 34.3 us -> 21.4 us
  Pallas kernels: 0 us -> 12 us
    reduce_scatter x1 -> x0, waiting for transfers between devices: 87.9 us -> none  [body(): lax.psum_scatter(jnp.dot(rows, w_out, preferred_element_type=jnp.float32)...]
    all_gather x2 -> x1, waiting for transfers between devices: 68.1 us -> 0.01 us  [body(): wq_all = lax.all_gather(w_query, ('zl', 'c'), axis=0, tiled=False)]
    ppermute x0 -> x13, waiting for transfers between devices: none -> 44.3 us  [the longest x6 30.8 us: shift_line(): return lax.ppermute(a, 'zl', [(i, (i + s) % ZL) for i in range(ZL)])]
    ppermute x0 -> x13, starting transfers between devices: none -> 26.3 us  [the longest x1 9.1 us: body(): wo_here = lax.ppermute(w_out, ('zl', 'c'), to_group)]
    dot_general x13 -> x10, matrix products: 30.8 us -> 17.6 us  [the longest x4 6.36 us: body(): jnp.dot(both, wq[h], preferred_element_type=jnp.float32)]
    pallas_call x0 -> x2, Pallas kernels: none -> 12 us  [the longest x1 10.2 us: body(): pl.pallas_call(lambda *refs: attention_kernel(*refs, pages=n_pages, fresh...]
    dynamic_slice x11 -> x2, local copies, waits for them, and re-layouts: 11 us -> 2.24 us  [the longest x1 1.66 us: body(): own_pages = lax.dynamic_index_in_dim(cache, c, 1, keepdims=True)]
    reduce_sum x7 -> x1, other arithmetic: 8.08 us -> 0.01 us  [body(): named = jnp.sum(matches.astype(jnp.float32), axis=1)]
  transfers between devices with their start and end apart: 5 -> 16, of which waited for: 5 -> 9; matrix products, arithmetic and copies ran while one was open for 2% -> 6% of each run, Pallas kernels for 0% -> 5%
where the time goes in v1:
time: 263 us; the launch traced here: 261 us
  waiting for transfers between devices  101 us (38%)
  blocking collectives  60.8 us (23%)
  starting transfers between devices  42.5 us (16%)
  matrix products  21.4 us (8%)
  between operations  14.3 us (5%)
  Pallas kernels  12 us (5%)
  other arithmetic  6.2 us (2%)
  local copies, waits for them, and re-layouts  3.19 us (1%)
    all_to_all x1, blocking collectives, body(): lax.all_to_all(outgoing.reshape(experts_all, CAP, width), ('y', 'zl', 'c'...  60.8 us
    all_to_all x1, waiting for transfers between devices, body(): lax.all_to_all(output.reshape(experts_all, CAP, width), ('y', 'zl', 'c'),...  49.6 us
    ppermute x6, waiting for transfers between devices, shift_line(): return lax.ppermute(a, 'zl', [(i, (i + s) % ZL) for i in range(ZL)])  30.8 us
    all_to_all x1, starting transfers between devices, body(): lax.all_to_all(own_pages, ('x', 'zh'), split_axis=0, concat_axis=2, tiled...  11.5 us
    ppermute x1, waiting for transfers between devices, body(): wo_here = lax.ppermute(w_out, ('zl', 'c'), to_group)  10.2 us
    pallas_call x1, Pallas kernels, body(): pl.pallas_call(lambda *refs: attention_kernel(*refs, pages=n_pages, fresh...  10.2 us
    ppermute x1, starting transfers between devices, body(): wo_here = lax.ppermute(w_out, ('zl', 'c'), to_group)  9.1 us
    ppermute x6, starting transfers between devices, shift_line(): return lax.ppermute(a, 'zl', [(i, (i + s) % ZL) for i in range(ZL)])  9.08 us
  transfers between devices with their start and end apart: 16, of which 9 were waited for; matrix products, arithmetic and copies ran while one was open for 6% of the time, Pallas kernels for 5%

profile of v1, /device:TPU:1, one launch (start us, length us, event | category | flops | bytes accessed | tf_op | source)
XLA Modules:
  0.0 261.2 jit_solution(1488583585753371193)
XLA Ops:
  7.2 0.0 copy-start
  7.2 0.0 all-gather.3.cloned.1.call-start
  7.2 0.7 all-gather.3.cloned.1.call-update
  7.9 1.7 constant_dynamic-slice_fusion
  9.6 11.5 %all-to-all-start = ((bf16[8,1,64,256]{3,2,1,0:T(8,128)(2,1)}), bf16[8,1,64,256]{3,2,1,0:T(8,128)(2,1)S(1)}, u32[]{:S(2)}, u32[]{:S(2)}) async-start(bf16[8,1,64,256]{3,2,1,0:T(8,128)(2,1)} %constant_dynamic-slice_fusion), calls=%async_computation | async-start | bytes 524288 | tf_op jit(solution)/shard_map/pages/all_to_all | solution.py:153
  21.1 1.2 fusion.14
  22.2 1.9 fusion.16
  24.1 1.0 collective-permute-start
  25.1 6.1 %all-to-all-done = bf16[8,1,64,256]{3,2,1,0:T(8,128)(2,1)S(1)} async-done(((bf16[8,1,64,256]{3,2,1,0:T(8,128)(2,1)}), bf16[8,1,64,256]{3,2,1,0:T(8,128)(2,1)S(1)}, u32[]{:S(2)}, u32[]{:S(2)}) %all-to-all-start) | async-done | bytes 262176 | tf_op jit(solution)/shard_map/pages/all_to_all | solution.py:153
  31.3 0.0 collective-permute-done
  31.3 1.7 constant_dynamic-update-slice_fusion.3
  33.0 0.0 copy-start.3
  33.0 4.2 %collective-permute-start.1 = (bf16[256,256]{1,0:T(8,128)(2,1)S(1)}, bf16[256,256]{1,0:T(8,128)(2,1)S(1)}, u32[]{:S(2)}, u32[]{:S(2)}) collective-permute-start(bf16[256,256]{1,0:T(8,128)(2,1)S(1)} %get-tuple-element.21), channel_id=1, source_target_pairs={{0,2},{2,4},{4,6},{6,0},{1,3},{3,5},{5,7},{7,1},{8,10},{10,12},{12... | collective-permute-start | bytes 393224 | tf_op jit(solution)/shard_map/keys/ppermute | solution.py:28
  37.2 0.8 collective-permute-start.2
  38.0 2.3 collective-permute-start.3
  40.3 1.9 collective-permute-done.1
  42.2 9.3 %collective-permute-done.2 = bf16[256,256]{1,0:T(8,128)(2,1)S(1)} collective-permute-done((bf16[256,256]{1,0:T(8,128)(2,1)S(1)}, bf16[256,256]{1,0:T(8,128)(2,1)S(1)}, u32[]{:S(2)}, u32[]{:S(2)}) %collective-permute-start.2) | collective-permute-done | bytes 131104 | tf_op jit(solution)/shard_map/keys/ppermute | solution.py:28
  51.5 1.3 collective-permute-done.3
  52.9 2.8 %collective-permute-start.4 = (bf16[1536,256]{1,0:T(8,128)(2,1)S(1)}, bf16[1536,256]{1,0:T(8,128)(2,1)}, u32[]{:S(2)}, u32[]{:S(2)}) collective-permute-start(bf16[1536,256]{1,0:T(8,128)(2,1)S(1)} %constant_dynamic-update-slice_fusion.refs_2_), channel_id=1, source_target_pairs={{0,8},{1,25},{8,16},{9,1},{16,24},{17,9},{24,0},{25,17},{2,10},{3,... | collective-permute-start | bytes 2359304 | tf_op jit(solution)/shard_map/keys/ppermute | solution.py:37
  55.7 9.1 %collective-permute-start.7 = (bf16[128,1536]{1,0:T(8,128)(2,1)}, bf16[128,1536]{1,0:T(8,128)(2,1)}, u32[]{:S(2)}, u32[]{:S(2)}) collective-permute-start(bf16[128,1536]{1,0:T(8,128)(2,1)} %param.19), channel_id=1, source_target_pairs={{0,0},{1,2},{2,4},{3,6},{4,1},{5,3},{6,5},{7,7},{8,8},{9,10},{10,1... | collective-permute-start | bytes 1179656 | tf_op jit(solution)/shard_map/weights/ppermute | solution.py:148
  64.8 1.4 collective-permute-start.5
  66.2 0.0 collective-permute-done.4.refs_3_
  66.2 1.9 collective-permute-start.6
  68.1 0.6 dynamic_slice.15
  68.7 0.6 pad_add_fusion.refs_0_.meta
  69.3 10.2 %collective-permute-done.7 = bf16[128,1536]{1,0:T(8,128)(2,1)} collective-permute-done((bf16[128,1536]{1,0:T(8,128)(2,1)}, bf16[128,1536]{1,0:T(8,128)(2,1)}, u32[]{:S(2)}, u32[]{:S(2)}) %collective-permute-start.7) | collective-permute-done | bytes 393248 | tf_op jit(solution)/shard_map/weights/ppermute | solution.py:148
  79.6 0.0 collective-permute-start.10
  79.6 1.8 collective-permute-start.9
  81.4 0.0 collective-permute-start.8
  81.4 1.6 convolution_convert_fusion.6
  83.0 1.6 convolution_convert_fusion.5
  84.6 1.6 convolution_convert_fusion.4
  86.2 1.6 convolution_convert_fusion.3
  87.8 0.0 collective-permute-done.5.refs_4_
  87.8 0.0 collective-permute-done.6.refs_5_
  87.8 10.2 %attention.1 = bf16[256,512]{1,0:T(8,128)(2,1)S(1)} custom-call(s32[4]{0:T(128)S(1)} %pad_add_fusion.refs_0_.meta, bf16[256,512]{1,0:T(8,128)(2,1)S(1)} %pad_maximum_fusion.2.refs_1_, bf16[1536,256]{1,0:T(8,128)(2,1)S(1)} %constant_dynamic-update-slice_fusion.refs_2_, bf16[1536,256]{1,0:T(8,128)(2,1)} %collective-permute-done.4.refs_3_, ...), custom_call_target="tpu_custom_call" | custom-call | flops 3221225472 | bytes 4194304 | tf_op jit(solution)/shard_map/attention/attention/pallas_call | solution.py:188
  98.1 0.0 copy-start.5
  98.1 0.0 copy-start.2
  98.1 0.0 collective-permute-done.10
  98.1 18.3 %collective-permute-done.9 = bf16[128,1536]{1,0:T(8,128)(2,1)} collective-permute-done((bf16[128,1536]{1,0:T(8,128)(2,1)}, bf16[128,1536]{1,0:T(8,128)(2,1)}, u32[]{:S(2)}, u32[]{:S(2)}) %collective-permute-start.9) | collective-permute-done | bytes 393248 | tf_op jit(solution)/shard_map/weights/ppermute | solution.py:28
  116.4 2.1 fusion.4
  118.5 0.0 copy-start.6
  118.5 0.0 copy-start.7
  118.5 0.1 slice.85
  118.6 0.7 collective-permute-start.11
  119.3 0.1 fusion.36
  119.4 1.8 collective-permute-done.11
  121.2 0.2 fusion.18
  121.5 0.3 fusion.34
  121.9 1.1 convolution_convert_fusion.1
  122.9 60.8 %all_to_all.19 = bf16[32,24,1536]{2,1,0:T(8,128)(2,1)S(1)} all-to-all(bf16[32,24,1536]{2,1,0:T(8,128)(2,1)S(1)} %bitcast.53), channel_id=1, replica_groups=mesh['x'=4,'zh'=2,'y'=4,'zl'=4,'c'=2] {'y','zl','c'}, dimensions={0} | all-to-all | bytes 4718592 | tf_op jit(solution)/shard_map/dispatch/all_to_all | solution.py:236
  183.8 3.8 %fusion = f32[768,1536]{1,0:T(8,128)S(1)} fusion(bf16[768,1536]{1,0:T(8,128)(2,1)S(1)} %bitcast.55, bf16[1,1536,1536]{2,1,0:T(8,128)(2,1)S(1)} %bitcast.58), kind=kOutput, calls=%fused_computation | convolution fusion | flops 3623878656 | bytes 11796480 | tf_op jit(solution)/shard_map/experts/dot_general | solution.py:259
  187.6 3.5 %convolution_convert_fusion = bf16[768,1536]{1,0:T(8,128)(2,1)} fusion(bf16[1,768,1536]{2,1,0:T(8,128)(2,1)S(1)} %copy-done, f32[768,1536]{1,0:T(8,128)S(1)} %fusion), kind=kOutput, calls=%fused_computation.2 | convolution fusion | flops 1814888448 | bytes 9437184 | tf_op jit(solution)/shard_map/experts/dot_general | solution.py:265
  191.0 4.7 %all-to-all-start.2 = ((bf16[32,24,1536]{2,1,0:T(8,128)(2,1)}), bf16[32,24,1536]{2,1,0:T(8,128)(2,1)}, u32[]{:S(2)}, u32[]{:S(2)}) async-start(bf16[32,24,1536]{2,1,0:T(8,128)(2,1)} %bitcast.54), calls=%async_computation.2 | async-start | bytes 4718592 | tf_op jit(solution)/shard_map/combine/all_to_all | solution.py:270
  195.8 0.8 pad_maximum_fusion.1.x_ref
  196.6 1.8 new_cache.1
  198.4 0.3 collective-permute-start.12
  198.7 1.5 collective-permute-done.12
  200.2 0.1 slice_select_fusion
  200.4 0.8 copy.18
  201.2 0.3 fusion.28
  201.4 49.6 %all-to-all-done.2 = bf16[32,24,1536]{2,1,0:T(8,128)(2,1)} async-done(((bf16[32,24,1536]{2,1,0:T(8,128)(2,1)}), bf16[32,24,1536]{2,1,0:T(8,128)(2,1)}, u32[]{:S(2)}, u32[]{:S(2)}) %all-to-all-start.2) | async-done | bytes 2359328 | tf_op jit(solution)/shard_map/combine/all_to_all | solution.py:270
  251.0 2.4 fusion.24
  253.5 0.9 fusion.21
  (34 shorter events, 0.3 us)
Async XLA Ops:
  7.2 180.4 %copy-start = (bf16[1,768,1536]{2,1,0:T(8,128)(2,1)S(1)}, bf16[1,768,1536]{2,1,0:T(8,128)(2,1)}, u32[]{:S(2)}) copy-start(bf16[1,768,1536]{2,1,0:T(8,128)(2,1)} %param.23) | copy-start | bytes 7077892
  7.2 74.2 %all-gather.3.cloned.1.call-start = ((), (), s32[]{:S(2)}) async-start(), calls=%async_computation.3 | async-start | bytes 3538944 | tf_op jit(solution)/shard_map/weights/all_gather | solution.py:143
  9.6 21.6 %all-to-all-start = ((bf16[8,1,64,256]{3,2,1,0:T(8,128)(2,1)}), bf16[8,1,64,256]{3,2,1,0:T(8,128)(2,1)S(1)}, u32[]{:S(2)}, u32[]{:S(2)}) async-start(bf16[8,1,64,256]{3,2,1,0:T(8,128)(2,1)} %constant_dynamic-slice_fusion), calls=%async_computation | async-start | bytes 524288 | tf_op jit(solution)/shard_map/pages/all_to_all | solution.py:153
  22.2 45.9 %copy-start.8 = (s32[8]{0:T(128)S(1)}, s32[8]{0:T(128)}, u32[]{:S(2)}) copy-start(s32[8]{0:T(128)} %param.14) | copy-start | bytes 100
  24.1 7.1 %collective-permute-start = (bf16[128,1536]{1,0:T(8,128)(2,1)}, bf16[128,1536]{1,0:T(8,128)(2,1)}, u32[]{:S(2)}, u32[]{:S(2)}) collective-permute-start(bf16[128,1536]{1,0:T(8,128)(2,1)} %fusion.16), channel_id=1, source_target_pairs={{0,1},{1,0},{2,3},{3,2},{4,5},{5,4},{6,7},{7,6},{8,9},{9,8},{10,11... | collective-permute-start | bytes 1179656 | tf_op jit(solution)/shard_map/keys/ppermute | solution.py:24
  33.0 33.2 %copy-start.3 = (bf16[256,256]{1,0:T(8,128)(2,1)}, bf16[256,256]{1,0:T(8,128)(2,1)S(1)}, u32[]{:S(2)}) copy-start(bf16[256,256]{1,0:T(8,128)(2,1)S(1)} %get-tuple-element.21) | copy-start | bytes 393220
  33.0 9.1 %collective-permute-start.1 = (bf16[256,256]{1,0:T(8,128)(2,1)S(1)}, bf16[256,256]{1,0:T(8,128)(2,1)S(1)}, u32[]{:S(2)}, u32[]{:S(2)}) collective-permute-start(bf16[256,256]{1,0:T(8,128)(2,1)S(1)} %get-tuple-element.21), channel_id=1, source_target_pairs={{0,2},{2,4},{4,6},{6,0},{1,3},{3,5},{5,7},{7,1},{8,10},{10,12},{12... | collective-permute-start | bytes 393224 | tf_op jit(solution)/shard_map/keys/ppermute | solution.py:28
  37.2 14.3 %collective-permute-start.2 = (bf16[256,256]{1,0:T(8,128)(2,1)S(1)}, bf16[256,256]{1,0:T(8,128)(2,1)S(1)}, u32[]{:S(2)}, u32[]{:S(2)}) collective-permute-start(bf16[256,256]{1,0:T(8,128)(2,1)S(1)} %get-tuple-element.21), channel_id=1, source_target_pairs={{0,4},{2,6},{4,0},{6,2},{1,5},{3,7},{5,1},{7,3},{8,12},{10,14},{12... | collective-permute-start | bytes 393224 | tf_op jit(solution)/shard_map/keys/ppermute | solution.py:28
  38.0 14.8 %collective-permute-start.3 = (bf16[256,256]{1,0:T(8,128)(2,1)S(1)}, bf16[256,256]{1,0:T(8,128)(2,1)S(1)}, u32[]{:S(2)}, u32[]{:S(2)}) collective-permute-start(bf16[256,256]{1,0:T(8,128)(2,1)S(1)} %get-tuple-element.21), channel_id=1, source_target_pairs={{0,6},{2,0},{4,2},{6,4},{1,7},{3,1},{5,3},{7,5},{8,14},{10,8},{12,... | collective-permute-start | bytes 393224 | tf_op jit(solution)/shard_map/keys/ppermute | solution.py:28
  52.9 13.3 %collective-permute-start.4 = (bf16[1536,256]{1,0:T(8,128)(2,1)S(1)}, bf16[1536,256]{1,0:T(8,128)(2,1)}, u32[]{:S(2)}, u32[]{:S(2)}) collective-permute-start(bf16[1536,256]{1,0:T(8,128)(2,1)S(1)} %constant_dynamic-update-slice_fusion.refs_2_), channel_id=1, source_target_pairs={{0,8},{1,25},{8,16},{9,1},{16,24},{17,9},{24,0},{25,17},{2,10},{3,... | collective-permute-start | bytes 2359304 | tf_op jit(solution)/shard_map/keys/ppermute | solution.py:37
  55.7 23.9 %collective-permute-start.7 = (bf16[128,1536]{1,0:T(8,128)(2,1)}, bf16[128,1536]{1,0:T(8,128)(2,1)}, u32[]{:S(2)}, u32[]{:S(2)}) collective-permute-start(bf16[128,1536]{1,0:T(8,128)(2,1)} %param.19), channel_id=1, source_target_pairs={{0,0},{1,2},{2,4},{3,6},{4,1},{5,3},{6,5},{7,7},{8,8},{9,10},{10,1... | collective-permute-start | bytes 1179656 | tf_op jit(solution)/shard_map/weights/ppermute | solution.py:148
  64.8 23.0 %collective-permute-start.5 = (bf16[1536,256]{1,0:T(8,128)(2,1)S(1)}, bf16[1536,256]{1,0:T(8,128)(2,1)}, u32[]{:S(2)}, u32[]{:S(2)}) collective-permute-start(bf16[1536,256]{1,0:T(8,128)(2,1)S(1)} %constant_dynamic-update-slice_fusion.refs_2_), channel_id=1, source_target_pairs={{0,24},{1,9},{8,0},{9,17},{16,8},{17,25},{24,16},{25,1},{2,26},{3,... | collective-permute-start | bytes 2359304 | tf_op jit(solution)/shard_map/keys/ppermute | solution.py:37
  66.2 21.6 %collective-permute-start.6 = (bf16[1536,256]{1,0:T(8,128)(2,1)}, bf16[1536,256]{1,0:T(8,128)(2,1)}, u32[]{:S(2)}, u32[]{:S(2)}) collective-permute-start(bf16[1536,256]{1,0:T(8,128)(2,1)} %collective-permute-done.4.refs_3_), channel_id=1, source_target_pairs={{0,8},{1,25},{8,16},{9,1},{16,24},{17,9},{24,0},{25,17},{2,10},{3,... | collective-permute-start | bytes 2359304 | tf_op jit(solution)/shard_map/keys/ppermute | solution.py:37
  69.3 18.5 %copy-start.1 = (s32[4]{0:T(128)}, s32[4]{0:T(128)S(1)}, u32[]{:S(2)}) copy-start(s32[4]{0:T(128)S(1)} %pad_add_fusion.refs_0_.meta) | copy-start | bytes 52
  79.6 18.5 %collective-permute-start.10 = (bf16[128,1536]{1,0:T(8,128)(2,1)}, bf16[128,1536]{1,0:T(8,128)(2,1)}, u32[]{:S(2)}, u32[]{:S(2)}) collective-permute-start(bf16[128,1536]{1,0:T(8,128)(2,1)} %collective-permute-done.7), channel_id=1, source_target_pairs={{0,6},{2,0},{4,2},{6,4},{1,7},{3,1},{5,3},{7,5},{8,14},{10,8},{12,... | collective-permute-start | bytes 1179656 | tf_op jit(solution)/shard_map/weights/ppermute | solution.py:28
  79.6 36.8 %collective-permute-start.9 = (bf16[128,1536]{1,0:T(8,128)(2,1)}, bf16[128,1536]{1,0:T(8,128)(2,1)}, u32[]{:S(2)}, u32[]{:S(2)}) collective-permute-start(bf16[128,1536]{1,0:T(8,128)(2,1)} %collective-permute-done.7), channel_id=1, source_target_pairs={{0,4},{2,6},{4,0},{6,2},{1,5},{3,7},{5,1},{7,3},{8,12},{10,14},{12... | collective-permute-start | bytes 1179656 | tf_op jit(solution)/shard_map/weights/ppermute | solution.py:28
  81.4 35.0 %collective-permute-start.8 = (bf16[128,1536]{1,0:T(8,128)(2,1)}, bf16[128,1536]{1,0:T(8,128)(2,1)}, u32[]{:S(2)}, u32[]{:S(2)}) collective-permute-start(bf16[128,1536]{1,0:T(8,128)(2,1)} %collective-permute-done.7), channel_id=1, source_target_pairs={{0,2},{2,4},{4,6},{6,0},{1,3},{3,5},{5,7},{7,1},{8,10},{10,12},{12... | collective-permute-start | bytes 1179656 | tf_op jit(solution)/shard_map/weights/ppermute | solution.py:28
  98.1 21.2 %copy-start.5 = (s32[128,4]{0,1:T(4,128)S(1)}, s32[128,4]{0,1:T(4,128)}, u32[]{:S(2)}) copy-start(s32[128,4]{0,1:T(4,128)} %param.13) | copy-start | bytes 6148
  98.1 23.1 %copy-start.2 = (bf16[128,1536]{1,0:T(8,128)(2,1)S(1)}, bf16[128,1536]{1,0:T(8,128)(2,1)}, u32[]{:S(2)}) copy-start(bf16[128,1536]{1,0:T(8,128)(2,1)} %param.12) | copy-start | bytes 1179652
  116.4 67.4 %slice-start = ((s8[4718592]{0:T(1024)(128)(4,1)}), s8[4194304]{0:T(1024)(128)(4,1)S(1)}, s32[]{:S(2)}) async-start(s8[4718592]{0:T(1024)(128)(4,1)} %bitcast.57), calls=%async_computation.4 | async-start | bytes 8388608
  118.5 3.0 %copy-start.6 = (f32[1536]{0:T(1024)S(1)}, f32[1536]{0:T(1024)}, u32[]{:S(2)}) copy-start(f32[1536]{0:T(1024)} %param.20) | copy-start | bytes 18436
  118.5 3.0 %copy-start.7 = (bf16[1536,32]{0,1:T(8,128)(2,1)S(1)}, bf16[1536,32]{0,1:T(8,128)(2,1)}, u32[]{:S(2)}) copy-start(bf16[1536,32]{0,1:T(8,128)(2,1)} %param.21) | copy-start | bytes 294916
  118.6 2.7 %collective-permute-start.11 = (f32[128,1536]{1,0:T(8,128)S(1)}, f32[128,1536]{1,0:T(8,128)S(1)}, u32[]{:S(2)}, u32[]{:S(2)}) collective-permute-start(f32[128,1536]{1,0:T(8,128)S(1)} %slice.85), channel_id=1, source_target_pairs={{0,1},{1,0},{2,3},{3,2},{4,5},{5,4},{6,7},{7,6},{8,9},{9,8},{10,11... | collective-permute-start | bytes 2359304 | tf_op jit(solution)/shard_map/out_projection/ppermute | solution.py:24
  119.4 64.3 %slice-start.1 = ((s8[4718592]{0:T(1024)(128)(4,1)}), s8[524288]{0:T(1024)(128)(4,1)S(1)}, s32[]{:S(2)}) async-start(s8[4718592]{0:T(1024)(128)(4,1)} %bitcast.57), calls=%async_computation.5 | async-start | bytes 1048576
  191.0 4.7 %copy-start.4 = (bf16[256,256]{1,0:T(8,128)(2,1)S(1)}, bf16[256,256]{1,0:T(8,128)(2,1)}, u32[]{:S(2)}) copy-start(bf16[256,256]{1,0:T(8,128)(2,1)} %copy-done.3) | copy-start | bytes 393220
  191.0 60.0 %all-to-all-start.2 = ((bf16[32,24,1536]{2,1,0:T(8,128)(2,1)}), bf16[32,24,1536]{2,1,0:T(8,128)(2,1)}, u32[]{:S(2)}, u32[]{:S(2)}) async-start(bf16[32,24,1536]{2,1,0:T(8,128)(2,1)} %bitcast.54), calls=%async_computation.2 | async-start | bytes 4718592 | tf_op jit(solution)/shard_map/combine/all_to_all | solution.py:270
  198.4 1.7 collective-permute-start.12
Sparse Core Ops, SparseCore 0:
  9.8 63.4 all-gather.2
